TPU v7x, 32 devices: a whole 2x2x4 slice. The times are simulated.
32 devices in a mesh: prow: 4 (over x, core), pcol: 8 (over z, y).
Axes of the slice: x: 2, y: 2, z: 4, core: 2. Of those that a mesh axis runs over, the one named last changes fastest.
Arguments:
- coords: int32 [3, 8192], P(None, ('prow', 'pcol')), may hold values from 0 to 1023
- block_map: int32 [64], replicated, may hold values from 0 to 63, each once
- pattern: int32 [2, 64], replicated, may hold values 0 or 1
Outputs:
- factor: float32 [16, 4, 128, 8, 8, 128], P(None, 'prow', None, None, 'pcol')
Inputs may be any that keep to these rules, and one draw needn't show every extreme that they name: `block_map`: every block number appears once.
All inputs are finite; a program needn't handle non-finite values.
Results may differ from a plain program's by a relative error of at most 0.0001.
Values sent between devices are 32-bit elements; how exact they have to be, the bound alone decides.
No kernel may reach another device: no remote copies, remote signals or barrier semaphores. Data moves between devices by JAX's collectives and lax.ppermute only.
A program may use at most 128 MiB of HBM per device.

v0:
```python
import jax
import jax.numpy as jnp
from jax import lax
from jax.sharding import PartitionSpec as P

BLOCK = 128
SNODE_BLOCKS = 4
PANELS = 2
spread_factor = 89.0
scale_gain = 8.0


def spread_2(value, axis, source):
    kept = jnp.where(lax.axis_index(axis) == source, value, 0).astype(value.dtype)
    return lax.psum(kept, axis)


def lookup(table, index):
    spots = jnp.arange(table.shape[-1], dtype=jnp.int32)
    return jnp.sum(jnp.where(index[..., None] == spots, table, 0), axis=-1)


def member(panel_at, ids, pattern):
    first = panel_at * SNODE_BLOCKS
    stop = first + SNODE_BLOCKS
    value = lookup(pattern[panel_at], ids)
    own = (ids >= first) & (ids < stop)
    before = ids < first
    return jnp.where(own, 1, jnp.where(before, 0, value)).astype(jnp.float32)


def block_mask(row_ids, col_ids, pattern):
    weight = (row_ids[:, None] == col_ids[None, :]).astype(jnp.float32)
    for panel_at in range(PANELS):
        row_in = member(panel_at, row_ids, pattern)
        col_in = member(panel_at, col_ids, pattern)
        weight = weight + row_in[:, None] * col_in[None, :]
    return weight


def wendland(dist_sq, radius):
    ratio = jnp.sqrt(dist_sq) / radius
    rest = jnp.maximum(1.0 - ratio, 0.0)
    rest_sq = rest * rest
    return rest_sq * rest_sq * rest_sq * ((35.0 * ratio + 18.0) * ratio + 3.0) * (1.0 / 3.0)


def local(coords, block_map, pattern):
    rows_n = lax.axis_size("prow")
    cols_n = lax.axis_size("pcol")
    prow_at = lax.axis_index("prow")
    pcol_at = lax.axis_index("pcol")
    nblocks = block_map.shape[0]
    row_count = nblocks // rows_n
    col_count = nblocks // cols_n
    front = nblocks * BLOCK
    width = SNODE_BLOCKS * BLOCK
    radius = (spread_factor / front) ** (1.0 / 3.0)
    all_points = lax.all_gather(coords, ("prow", "pcol"), axis=1, tiled=True)
    inverse = (
        jnp.zeros((nblocks,), jnp.int32).at[block_map].set(jnp.arange(nblocks, dtype=jnp.int32))
    )
    placed = all_points.reshape(3, nblocks, BLOCK)[:, inverse, :]
    points = placed.astype(jnp.float32) * (1.0 / 1024.0)
    row_pts = lax.dynamic_index_in_dim(
        points.reshape(3, row_count, rows_n, BLOCK), prow_at, 2, keepdims=False
    )
    col_pts = lax.dynamic_index_in_dim(
        points.reshape(3, col_count, cols_n, BLOCK), pcol_at, 2, keepdims=False
    )
    row_ids = jnp.arange(row_count, dtype=jnp.int32) * rows_n + prow_at
    col_ids = jnp.arange(col_count, dtype=jnp.int32) * cols_n + pcol_at
    dist = (row_pts[0][:, :, None, None] - col_pts[0][None, None, :, :]) ** 2
    dist = dist + (row_pts[1][:, :, None, None] - col_pts[1][None, None, :, :]) ** 2
    dist = dist + (row_pts[2][:, :, None, None] - col_pts[2][None, None, :, :]) ** 2
    mask = block_mask(row_ids, col_ids, pattern)
    coupling = wendland(dist, radius) * mask[:, None, :, None]
    row_part = jnp.sum(coupling, axis=(2, 3))
    col_part = jnp.sum(coupling, axis=(0, 1))
    row_total = lax.psum(row_part, "pcol")
    col_total = lax.psum(col_part, "prow")
    row_scale = scale_gain * lax.rsqrt(1.0 + row_total)
    col_scale = scale_gain * lax.rsqrt(1.0 + col_total)
    same_block = (row_ids[:, None] == col_ids[None, :])[:, None, :, None]
    same_cell = (jnp.arange(BLOCK)[:, None] == jnp.arange(BLOCK)[None, :])[None, :, None, :]
    matrix = coupling * row_scale[:, :, None, None] * col_scale[None, None, :, :]
    matrix = matrix + (same_block & same_cell).astype(jnp.float32)
    for panel_at in range(PANELS):
        first = panel_at * SNODE_BLOCKS
        stop = first + SNODE_BLOCKS
        owner_block = first // cols_n
        column_piece = matrix[:, :, owner_block, :]
        spread = lax.all_gather(column_piece, "pcol", axis=2, tiled=True)
        begin = first % cols_n * BLOCK
        panel = spread[:, :, begin : begin + width]
        offset = (prow_at - first) % rows_n
        valid = (offset < SNODE_BLOCKS).astype(jnp.float32)
        local_row = jnp.minimum((first + offset) // rows_n, row_count - 1)
        piece = lax.dynamic_index_in_dim(panel, local_row, 0, keepdims=False) * valid
        stacked = lax.all_gather(piece, "prow", axis=0, tiled=True)
        diagonal = jnp.concatenate(
            [
                stacked[(first + step) % rows_n * BLOCK : ((first + step) % rows_n + 1) * BLOCK]
                for step in range(SNODE_BLOCKS)
            ],
            axis=0,
        )
        lower = jnp.linalg.cholesky(diagonal)
        flat = panel.reshape(row_count * BLOCK, width)
        solved = lax.linalg.triangular_solve(
            lower, flat, left_side=False, lower=True, transpose_a=True
        )
        factor_rows = (
            solved.reshape(row_count, BLOCK, width)
            * (row_ids >= first).astype(jnp.float32)[:, None, None]
        )
        trail_rows = factor_rows * (row_ids >= stop).astype(jnp.float32)[:, None, None]
        chosen = factor_rows[col_ids // rows_n]
        root = pcol_at % rows_n
        col_rows = spread_2(chosen, "prow", root)
        col_trail = col_rows * (col_ids >= stop).astype(jnp.float32)[:, None, None]
        update = jnp.einsum("aik,cjk->aicj", trail_rows, col_trail, precision=lax.Precision.HIGHEST)
        matrix = matrix - update
        in_panel = (col_ids >= first) & (col_ids < stop)
        which = jnp.clip(col_ids - first, 0, SNODE_BLOCKS - 1)
        taken = jnp.take(factor_rows.reshape(row_count, BLOCK, SNODE_BLOCKS, BLOCK), which, axis=2)
        matrix = jnp.where(in_panel[None, None, :, None], taken, matrix)
        row_in = (row_ids >= first) & (row_ids < stop)
        upper = row_in[:, None] & (col_ids >= stop)[None, :]
        matrix = jnp.where(upper[:, None, :, None], 0.0, matrix)
    return matrix.reshape(row_count, 1, BLOCK, col_count, 1, BLOCK)


def solution(mesh):
    placed = (P(None, ("prow", "pcol")), P(), P())
    return jax.shard_map(
        local,
        mesh=mesh,
        in_specs=placed,
        out_specs=P(None, "prow", None, None, "pcol", None),
        check_vma=False,
    )
```

profile of v0, /device:TPU:0, one launch (start us, length us, event | category | flops | bytes accessed | tf_op | source)
XLA Modules:
  0.0 940.7 jit_solution(6668163431641681821)
XLA Ops:
  8.0 70.7 %all_gather.15 = s32[3,8192]{1,0:T(4,128)S(1)} all-gather(s32[3,256]{1,0:T(4,128)} %param.8), channel_id=1, replica_groups=mesh['prow'=4,'pcol'=8] {'prow','pcol'}, dimensions={1}, use_global_device_ids=true | all-gather | bytes 101376 | tf_op jit(solution)/shard_map/all_gather | solution.py:59
  89.5 17.4 %psum.28 = f32[16,128]{1,0:T(8,128)S(1)} all-reduce(f32[16,128]{1,0:T(8,128)S(1)} %get-tuple-element.24), channel_id=1, replica_groups=mesh['prow'=4,'pcol'=8] {'pcol'}, use_global_device_ids=true, to_apply=%region_6.7 | all-reduce | flops 2048 | bytes 16384 | tf_op jit(solution)/shard_map/psum | solution.py:80
  112.9 9.8 %convert_add_fusion = f32[16,128,8,128]{1,3,0,2:T(8,128)S(1)} fusion(f32[8,128]{1,0:T(8,128)S(1)} %rsqrt_multiply_fusion.1, f32[16,128]{1,0:T(8,128)S(1)} %rsqrt_multiply_fusion, f32[16,8]{0,1:T(8,128)S(1)} %add_multiply_fusion, f32[8,128]{1,0:T(8,128)S(1)} %bitcast.216, f32[16,128]{1,0:T(8,128)S(1)} %bitcast.207, f32[8,128]{1,0:T(8,128)S(1)} %bitcast.213, ...), kind=kLoop, calls=%fused_computation.18 | loop fusion | flops 52428800 | bytes 8454784 | tf_op jit(solution)/shard_map/add | solution.py:87
  123.9 122.2 %all-gather.9.cloned.1.call-done = f32[16,128,1,1024]{1,3,0,2:T(8,128)} async-done(((f32[16,128,1,128]{1,3,0,2:T(8,128)}), f32[16,128,1,1024]{1,3,0,2:T(8,128)}) %all-gather.9.cloned.1.call-update) | async-done | bytes 8388624 | tf_op jit(solution)/shard_map/all_gather | solution.py:93
  269.6 11.7 %cholesky.286 = f32[128,128]{1,0:T(8,128)S(1)} custom-call(f32[128,128]{1,0:T(8,128)S(1)} %cholesky.426), custom_call_target="Cholesky" | custom-call | tf_op jit(solution)/shard_map/jit(cholesky)/cholesky | solution.py:108
  281.5 9.8 %custom-call.27 = f32[1,128,128]{1,2,0:T(8,128)S(1)} custom-call(f32[1,128,128]{2,1,0:T(8,128)S(1)} %get-tuple-element.79), custom_call_target="InvertDiagBlocksLowerTriangular" | custom-call | tf_op jit(solution)/shard_map/jit(cholesky)/cholesky | solution.py:108
  292.0 11.7 %cholesky.305 = f32[128,128]{1,0:T(8,128)S(1)} custom-call(f32[128,128]{1,0:T(8,128)S(1)} %cholesky.430), custom_call_target="Cholesky" | custom-call | tf_op jit(solution)/shard_map/jit(cholesky)/cholesky | solution.py:108
  305.0 10.2 %custom-call.28 = f32[1,128,128]{1,2,0:T(8,128)S(1)} custom-call(f32[1,128,128]{2,1,0:T(8,128)S(1)} %get-tuple-element.76), custom_call_target="InvertDiagBlocksLowerTriangular" | custom-call | tf_op jit(solution)/shard_map/jit(cholesky)/cholesky | solution.py:108
  315.9 11.7 %cholesky.326 = f32[128,128]{1,0:T(8,128)S(1)} custom-call(f32[128,128]{1,0:T(8,128)S(1)} %cholesky.435), custom_call_target="Cholesky" | custom-call | tf_op jit(solution)/shard_map/jit(cholesky)/cholesky | solution.py:108
  338.7 11.7 %cholesky.343 = f32[128,128]{1,0:T(8,128)S(1)} custom-call(f32[128,128]{1,0:T(8,128)S(1)} %convolution_subtract_fusion.9), custom_call_target="Cholesky" | custom-call | tf_op jit(solution)/shard_map/jit(cholesky)/cholesky | solution.py:108
  362.0 39.3 %custom-call.30 = f32[4,128,128]{1,2,0:T(8,128)S(1)} custom-call(f32[4,128,128]{2,1,0:T(8,128)S(1)} %get-tuple-element.22), custom_call_target="InvertDiagBlocksLowerTriangular" | custom-call | tf_op jit(solution)/shard_map/triangular_solve/custom-call.3 | solution.py:110
  472.0 20.2 %all-reduce.4.cloned.1.call-done = f32[8,128,512]{2,1,0:T(8,128)} async-done(((f32[8,128,512]{2,1,0:T(8,128)}), f32[8,128,512]{2,1,0:T(8,128)}) %all-reduce.4.cloned.1.call-update) | async-done | bytes 2097168 | tf_op jit(solution)/shard_map/psum | solution.py:15
  492.2 26.2 %fusion.4 = f32[16,128,8,128]{1,3,0,2:T(8,128)S(1)} fusion(f32[8,16,128,128]{2,3,1,0:T(8,128)} %copy.31, pred[8]{0:T(512)(128)(4,1)S(1)} %get-tuple-element.88, pred[8]{0:T(512)(128)(4,1)S(1)} %get-tuple-element.89, pred[16,8]{0,1:T(8,128)(4,1)S(1)} %broadcast_and_fusion, f32[8,128,512]{2,1,0:T(8,128)} %all-reduce.4.cloned.1.call-done, ...), kind=kOutput, calls=%fused_computation.17 | convolution fusion | flops 12947292160 | bytes 23135088 | tf_op jit(solution)/shard_map/aik,cjk->aicj/dot_general | solution.py:122
  522.9 124.6 %all-gather.13.cloned.1.call-done = f32[16,128,1,1024]{1,3,0,2:T(8,128)} async-done(((f32[16,128,1,128]{1,3,0,2:T(8,128)}), f32[16,128,1,1024]{1,3,0,2:T(8,128)}) %all-gather.13.cloned.1.call-update) | async-done | bytes 8388624 | tf_op jit(solution)/shard_map/all_gather | solution.py:93
  670.9 11.7 %cholesky.358 = f32[128,128]{1,0:T(8,128)S(1)} custom-call(f32[128,128]{1,0:T(8,128)S(1)} %cholesky.439), custom_call_target="Cholesky" | custom-call | tf_op jit(solution)/shard_map/jit(cholesky)/cholesky | solution.py:108
  682.8 9.8 %custom-call.31 = f32[1,128,128]{1,2,0:T(8,128)S(1)} custom-call(f32[1,128,128]{2,1,0:T(8,128)S(1)} %get-tuple-element.69), custom_call_target="InvertDiagBlocksLowerTriangular" | custom-call | tf_op jit(solution)/shard_map/jit(cholesky)/cholesky | solution.py:108
  693.3 11.7 %cholesky.377 = f32[128,128]{1,0:T(8,128)S(1)} custom-call(f32[128,128]{1,0:T(8,128)S(1)} %cholesky.443), custom_call_target="Cholesky" | custom-call | tf_op jit(solution)/shard_map/jit(cholesky)/cholesky | solution.py:108
  706.3 10.2 %custom-call.32 = f32[1,128,128]{1,2,0:T(8,128)S(1)} custom-call(f32[1,128,128]{2,1,0:T(8,128)S(1)} %get-tuple-element.66), custom_call_target="InvertDiagBlocksLowerTriangular" | custom-call | tf_op jit(solution)/shard_map/jit(cholesky)/cholesky | solution.py:108
  717.2 11.7 %cholesky.398 = f32[128,128]{1,0:T(8,128)S(1)} custom-call(f32[128,128]{1,0:T(8,128)S(1)} %cholesky.448), custom_call_target="Cholesky" | custom-call | tf_op jit(solution)/shard_map/jit(cholesky)/cholesky | solution.py:108
  740.1 11.7 %cholesky.415 = f32[128,128]{1,0:T(8,128)S(1)} custom-call(f32[128,128]{1,0:T(8,128)S(1)} %convolution_subtract_fusion.8), custom_call_target="Cholesky" | custom-call | tf_op jit(solution)/shard_map/jit(cholesky)/cholesky | solution.py:108
  763.3 39.3 %custom-call.34 = f32[4,128,128]{1,2,0:T(8,128)S(1)} custom-call(f32[4,128,128]{2,1,0:T(8,128)S(1)} %get-tuple-element.23), custom_call_target="InvertDiagBlocksLowerTriangular" | custom-call | tf_op jit(solution)/shard_map/triangular_solve/custom-call.3 | solution.py:110
  873.5 20.2 %all-reduce.6.cloned.1.call-done = f32[8,128,512]{2,1,0:T(8,128)} async-done(((f32[8,128,512]{2,1,0:T(8,128)}), f32[8,128,512]{2,1,0:T(8,128)}) %all-reduce.6.cloned.1.call-update) | async-done | bytes 2097168 | tf_op jit(solution)/shard_map/psum | solution.py:15
  893.6 19.5 %fusion.3 = f32[16,1,128,8,1,128]{2,5,0,3,4,1:T(8,128)} fusion(f32[8,16,128,128]{2,3,1,0:T(8,128)} %copy.37, f32[16,128,8,128]{1,3,0,2:T(8,128)} %copy-done.2, pred[8]{0:T(512)(128)(4,1)S(1)} %get-tuple-element.94, pred[8]{0:T(512)(128)(4,1)S(1)} %get-tuple-element.95, pred[16,8]{0,1:T(8,128)(4,1)S(1)} %broadcast_and_fusion.1, ...), kind=kOutput, calls=%fused_computation.15 | convolution fusion | flops 12894863360 | bytes 31457520 | tf_op jit(solution)/shard_map/aik,cjk->aicj/dot_general | solution.py:122
  913.1 20.5 %copy.40 = f32[16,1,128,8,1,128]{5,4,3,2,1,0:T(1,128)} copy(f32[16,1,128,8,1,128]{2,5,0,3,4,1:T(8,128)} %fusion.3) | data formatting | bytes 16777216 | tf_op jit(solution)/shard_map/reshape | solution.py:131
  (175 shorter events, 273.1 us)
Async XLA Ops:
  6.5 239.6 %all-gather.9.cloned.1.call-start = ((), (), s32[]{:S(2)}) async-start(), calls=%async_computation.2 | async-start | bytes 9437184 | tf_op jit(solution)/shard_map/all_gather | solution.py:93
  123.8 142.7 %all-gather.11.cloned.1.call-start = ((), (), s32[]{:S(2)}) async-start(), calls=%async_computation.3 | async-start | bytes 1310720 | tf_op jit(solution)/shard_map/all_gather | solution.py:100
  248.6 2.0 copy-start
  251.4 240.8 %all-reduce.4.cloned.1.call-start = ((), (), s32[]{:S(2)}) async-start(), calls=%async_computation | async-start | bytes 4194304 | tf_op jit(solution)/shard_map/psum | solution.py:15
  440.7 206.8 %all-gather.13.cloned.1.call-start = ((), (), s32[]{:S(2)}) async-start(), calls=%async_computation.4 | async-start | bytes 9437184 | tf_op jit(solution)/shard_map/all_gather | solution.py:93
  518.5 3.2 copy-start.2
  522.8 145.1 %all-gather.15.cloned.1.call-start = ((), (), s32[]{:S(2)}) async-start(), calls=%async_computation.5 | async-start | bytes 1310720 | tf_op jit(solution)/shard_map/all_gather | solution.py:100
  650.0 2.0 copy-start.1
  652.7 240.9 %all-reduce.6.cloned.1.call-start = ((), (), s32[]{:S(2)}) async-start(), calls=%async_computation.1 | async-start | bytes 4194304 | tf_op jit(solution)/shard_map/psum | solution.py:15
Sparse Core Ops, SparseCore 0:
  124.0 122.1 all-gather.8
  251.5 14.9 all-gather.10
  440.8 51.3 all-reduce.3
  522.9 124.5 all-gather.12
  652.8 14.9 all-gather.14
  842.2 51.3 all-reduce.5
where the time goes:
time: 950 us; the launch traced here: 941 us
  waiting for transfers between devices  306 us (32%)
  other arithmetic  294 us (31%)
  local copies, waits for them, and re-layouts  136 us (14%)
  blocking collectives  94.1 us (10%)
  matrix products  89.9 us (9%)
  between operations  19.6 us (2%)
    all_gather x2, waiting for transfers between devices, local(): spread = lax.all_gather(column_piece, 'pcol', axis=2, tiled=True)  247 us
    another operation x30, other arithmetic, local(): lower = jnp.linalg.cholesky(diagonal)  159 us
    another operation x7, other arithmetic, local(): lax.linalg.triangular_solve(lower, flat, left_side=False, lower=True, tra...  88 us
    all_gather x1, blocking collectives, local(): all_points = lax.all_gather(coords, ('prow', 'pcol'), axis=1, tiled=True)  70.7 us
    dot_general x2, matrix products, local(): jnp.einsum('aik,cjk->aicj', trail_rows, col_trail, precision=lax.Precisio...  45.7 us
    another operation x14, matrix products, local(): lax.linalg.triangular_solve(lower, flat, left_side=False, lower=True, tra...  40.5 us
    psum x2, waiting for transfers between devices, spread_2(): return lax.psum(kept, axis)  40.3 us
    gather x4, local copies, waits for them, and re-layouts, local(): jnp.take(factor_rows.reshape(row_count, BLOCK, SNODE_BLOCKS, BLOCK), whic...  31.8 us
  transfers between devices with their start and end apart: 6, of which 6 were waited for; matrix products, arithmetic and copies ran while one was open for 8% of the time, Pallas kernels for 0%

commit v1 on v0

--- a/solution.py
+++ b/solution.py
@@ -90,7 +90,24 @@
         stop = first + SNODE_BLOCKS
         owner_block = first // cols_n
         column_piece = matrix[:, :, owner_block, :]
-        spread = lax.all_gather(column_piece, "pcol", axis=2, tiled=True)
+        ways, here, k = (lax.axis_size("pcol"), lax.axis_index("pcol"), column_piece.shape[2])
+        lengths = [n * ways if d == 2 else n for d, n in enumerate(column_piece.shape)]
+        spread = lax.dynamic_update_slice_in_dim(
+            jnp.zeros(lengths, column_piece.dtype), column_piece, here * k, axis=2
+        )
+        going_up = going_down = column_piece
+        for far in range(1, ways // 2 + 1):
+            going_up = lax.ppermute(going_up, "pcol", [(d, (d + 1) % ways) for d in range(ways)])
+            spread = lax.dynamic_update_slice_in_dim(
+                spread, going_up, (here - far) % ways * k, axis=2
+            )
+            if 2 * far < ways:
+                going_down = lax.ppermute(
+                    going_down, "pcol", [(d, (d - 1) % ways) for d in range(ways)]
+                )
+                spread = lax.dynamic_update_slice_in_dim(
+                    spread, going_down, (here + far) % ways * k, axis=2
+                )
         begin = first % cols_n * BLOCK
         panel = spread[:, :, begin : begin + width]
         offset = (prow_at - first) % rows_n

time: 950 us -> 1030 us (1.084)
  waiting for transfers between devices: 306 us -> 342 us
  starting transfers between devices: 0.21 us -> 34.7 us
    ppermute x0 -> x14, waiting for transfers between devices: none -> 284 us  [the longest x8 284 us: local(): lax.ppermute(going_up, 'pcol', [(d, (d + 1) % ways) for d in range(ways)])]
    all_gather x2 -> x0, waiting for transfers between devices: 247 us -> none  [local(): spread = lax.all_gather(column_piece, 'pcol', axis=2, tiled=True)]
    ppermute x0 -> x14, starting transfers between devices: none -> 34.6 us  [the longest x8 18.5 us: local(): lax.ppermute(going_up, 'pcol', [(d, (d + 1) % ways) for d in range(ways)])]
    dynamic_update_slice x0 -> x16, local copies, waits for them, and re-layouts: none -> 11.2 us  [the longest x6 5.41 us: local(): lax.dynamic_update_slice_in_dim(spread, going_down, (here + far) % ways *...]
    unnamed x8 -> x14, local copies, waits for them, and re-layouts: 17.5 us -> 21 us
  transfers between devices with their start and end apart: 6 -> 18, of which waited for: 6 -> 12; matrix products, arithmetic and copies ran while one was open for 8% -> 8% of each run, Pallas kernels for 0% -> 0%
where the time goes in v1:
time: 1030 us; the launch traced here: 1020 us
  waiting for transfers between devices  342 us (33%)
  other arithmetic  294 us (29%)
  local copies, waits for them, and re-layouts  146 us (14%)
  blocking collectives  94.1 us (9%)
  matrix products  85.6 us (8%)
  starting transfers between devices  34.7 us (3%)
  between operations  19.5 us (2%)
    ppermute x8, waiting for transfers between devices, local(): lax.ppermute(going_up, 'pcol', [(d, (d + 1) % ways) for d in range(ways)])  284 us
    another operation x30, other arithmetic, local(): lower = jnp.linalg.cholesky(diagonal)  159 us
    another operation x7, other arithmetic, local(): lax.linalg.triangular_solve(lower, flat, left_side=False, lower=True, tra...  87.8 us
    all_gather x1, blocking collectives, local(): all_points = lax.all_gather(coords, ('prow', 'pcol'), axis=1, tiled=True)  70.7 us
    dot_general x2, matrix products, local(): jnp.einsum('aik,cjk->aicj', trail_rows, col_trail, precision=lax.Precisio...  45.7 us
    psum x2, waiting for transfers between devices, spread_2(): return lax.psum(kept, axis)  40.6 us
    another operation x14, matrix products, local(): lax.linalg.triangular_solve(lower, flat, left_side=False, lower=True, tra...  36.1 us
    gather x4, local copies, waits for them, and re-layouts, local(): jnp.take(factor_rows.reshape(row_count, BLOCK, SNODE_BLOCKS, BLOCK), whic...  31.6 us
  transfers between devices with their start and end apart: 18, of which 12 were waited for; matrix products, arithmetic and copies ran while one was open for 8% of the time, Pallas kernels for 0%

profile of v1, /device:TPU:0, one launch (start us, length us, event | category | flops | bytes accessed | tf_op | source)
XLA Modules:
  0.0 1015.9 jit_solution(16663552562091835902)
XLA Ops:
  8.0 70.7 %all_gather.9 = s32[3,8192]{1,0:T(4,128)S(1)} all-gather(s32[3,256]{1,0:T(4,128)} %param.8), channel_id=1, replica_groups=mesh['prow'=4,'pcol'=8] {'prow','pcol'}, dimensions={1}, use_global_device_ids=true | all-gather | bytes 101376 | tf_op jit(solution)/shard_map/all_gather | solution.py:59
  89.5 17.4 %psum.28 = f32[16,128]{1,0:T(8,128)S(1)} all-reduce(f32[16,128]{1,0:T(8,128)S(1)} %get-tuple-element.24), channel_id=1, replica_groups=mesh['prow'=4,'pcol'=8] {'pcol'}, use_global_device_ids=true, to_apply=%region_6.7 | all-reduce | flops 2048 | bytes 16384 | tf_op jit(solution)/shard_map/psum | solution.py:80
  131.0 41.9 %collective-permute-done = f32[16,128,128]{1,2,0:T(8,128)S(1)} collective-permute-done((f32[16,128,128]{1,2,0:T(8,128)S(1)}, f32[16,128,128]{1,2,0:T(8,128)S(1)}, u32[]{:S(2)}, u32[]{:S(2)}) %collective-permute-start) | collective-permute-done | bytes 1048608 | tf_op jit(solution)/shard_map/ppermute | solution.py:100
  177.6 41.9 %collective-permute-done.2 = f32[16,128,128]{1,2,0:T(8,128)S(1)} collective-permute-done((f32[16,128,128]{1,2,0:T(8,128)S(1)}, f32[16,128,128]{1,2,0:T(8,128)S(1)}, u32[]{:S(2)}, u32[]{:S(2)}) %collective-permute-start.2) | collective-permute-done | bytes 1048608 | tf_op jit(solution)/shard_map/ppermute | solution.py:100
  224.2 41.9 %collective-permute-done.4 = f32[16,128,128]{1,2,0:T(8,128)} collective-permute-done((f32[16,128,128]{1,2,0:T(8,128)S(1)}, f32[16,128,128]{1,2,0:T(8,128)}, u32[]{:S(2)}, u32[]{:S(2)}) %collective-permute-start.4) | collective-permute-done | bytes 1048608 | tf_op jit(solution)/shard_map/ppermute | solution.py:100
  275.1 17.9 %collective-permute-done.6 = f32[16,128,128]{1,2,0:T(8,128)S(1)} collective-permute-done((f32[16,128,128]{1,2,0:T(8,128)}, f32[16,128,128]{1,2,0:T(8,128)S(1)}, u32[]{:S(2)}, u32[]{:S(2)}) %collective-permute-start.6) | collective-permute-done | bytes 1048608 | tf_op jit(solution)/shard_map/ppermute | solution.py:100
  312.6 11.7 %cholesky.286 = f32[128,128]{1,0:T(8,128)S(1)} custom-call(f32[128,128]{1,0:T(8,128)S(1)} %cholesky.426), custom_call_target="Cholesky" | custom-call | tf_op jit(solution)/shard_map/jit(cholesky)/cholesky | solution.py:125
  334.9 11.7 %cholesky.305 = f32[128,128]{1,0:T(8,128)S(1)} custom-call(f32[128,128]{1,0:T(8,128)S(1)} %cholesky.430), custom_call_target="Cholesky" | custom-call | tf_op jit(solution)/shard_map/jit(cholesky)/cholesky | solution.py:125
  358.9 11.7 %cholesky.326 = f32[128,128]{1,0:T(8,128)S(1)} custom-call(f32[128,128]{1,0:T(8,128)S(1)} %cholesky.435), custom_call_target="Cholesky" | custom-call | tf_op jit(solution)/shard_map/jit(cholesky)/cholesky | solution.py:125
  381.7 11.7 %cholesky.343 = f32[128,128]{1,0:T(8,128)S(1)} custom-call(f32[128,128]{1,0:T(8,128)S(1)} %convolution_subtract_fusion.5), custom_call_target="Cholesky" | custom-call | tf_op jit(solution)/shard_map/jit(cholesky)/cholesky | solution.py:125
  405.0 39.3 %custom-call.30 = f32[4,128,128]{1,2,0:T(8,128)S(1)} custom-call(f32[4,128,128]{2,1,0:T(8,128)S(1)} %get-tuple-element.22), custom_call_target="InvertDiagBlocksLowerTriangular" | custom-call | tf_op jit(solution)/shard_map/triangular_solve/custom-call.3 | solution.py:127
  512.9 20.2 %all-reduce.4.cloned.1.call-done = f32[8,128,512]{2,1,0:T(8,128)} async-done(((f32[8,128,512]{2,1,0:T(8,128)}), f32[8,128,512]{2,1,0:T(8,128)}) %all-reduce.4.cloned.1.call-update) | async-done | bytes 2097168 | tf_op jit(solution)/shard_map/psum | solution.py:15
  533.1 26.2 %fusion.4 = f32[16,128,8,128]{1,3,0,2:T(8,128)S(1)} fusion(f32[8,16,128,128]{2,3,1,0:T(8,128)} %copy.31, pred[8]{0:T(512)(128)(4,1)S(1)} %get-tuple-element.90, pred[8]{0:T(512)(128)(4,1)S(1)} %get-tuple-element.91, pred[16,8]{0,1:T(8,128)(4,1)S(1)} %broadcast_and_fusion, f32[8,128,512]{2,1,0:T(8,128)} %all-reduce.4.cloned.1.call-done, ...), kind=kOutput, calls=%fused_computation.17 | convolution fusion | flops 12947292160 | bytes 23135088 | tf_op jit(solution)/shard_map/aik,cjk->aicj/dot_general | solution.py:139
  567.7 41.4 %collective-permute-done.7 = f32[16,128,128]{1,2,0:T(8,128)S(1)} collective-permute-done((f32[16,128,128]{1,2,0:T(8,128)S(1)}, f32[16,128,128]{1,2,0:T(8,128)S(1)}, u32[]{:S(2)}, u32[]{:S(2)}) %collective-permute-start.7) | collective-permute-done | bytes 1048608 | tf_op jit(solution)/shard_map/ppermute | solution.py:100
  614.3 41.0 %collective-permute-done.9 = f32[16,128,128]{1,2,0:T(8,128)} collective-permute-done((f32[16,128,128]{1,2,0:T(8,128)S(1)}, f32[16,128,128]{1,2,0:T(8,128)}, u32[]{:S(2)}, u32[]{:S(2)}) %collective-permute-start.9) | collective-permute-done | bytes 1048608 | tf_op jit(solution)/shard_map/ppermute | solution.py:100
  660.7 40.7 %collective-permute-done.11 = f32[16,128,128]{1,2,0:T(8,128)S(1)} collective-permute-done((f32[16,128,128]{1,2,0:T(8,128)}, f32[16,128,128]{1,2,0:T(8,128)S(1)}, u32[]{:S(2)}, u32[]{:S(2)}) %collective-permute-start.11) | collective-permute-done | bytes 1048608 | tf_op jit(solution)/shard_map/ppermute | solution.py:100
  710.2 17.5 %collective-permute-done.13 = f32[16,128,128]{1,2,0:T(8,128)S(1)} collective-permute-done((f32[16,128,128]{1,2,0:T(8,128)S(1)}, f32[16,128,128]{1,2,0:T(8,128)S(1)}, u32[]{:S(2)}, u32[]{:S(2)}) %collective-permute-start.13) | collective-permute-done | bytes 1048608 | tf_op jit(solution)/shard_map/ppermute | solution.py:100
  748.8 11.7 %cholesky.358 = f32[128,128]{1,0:T(8,128)S(1)} custom-call(f32[128,128]{1,0:T(8,128)S(1)} %cholesky.439), custom_call_target="Cholesky" | custom-call | tf_op jit(solution)/shard_map/jit(cholesky)/cholesky | solution.py:125
  771.2 11.7 %cholesky.377 = f32[128,128]{1,0:T(8,128)S(1)} custom-call(f32[128,128]{1,0:T(8,128)S(1)} %cholesky.443), custom_call_target="Cholesky" | custom-call | tf_op jit(solution)/shard_map/jit(cholesky)/cholesky | solution.py:125
  818.0 11.7 %cholesky.415 = f32[128,128]{1,0:T(8,128)S(1)} custom-call(f32[128,128]{1,0:T(8,128)S(1)} %convolution_subtract_fusion.4), custom_call_target="Cholesky" | custom-call | tf_op jit(solution)/shard_map/jit(cholesky)/cholesky | solution.py:125
  841.0 39.3 %custom-call.34 = f32[4,128,128]{1,2,0:T(8,128)S(1)} custom-call(f32[4,128,128]{2,1,0:T(8,128)S(1)} %get-tuple-element.23), custom_call_target="InvertDiagBlocksLowerTriangular" | custom-call | tf_op jit(solution)/shard_map/triangular_solve/custom-call.3 | solution.py:127
  948.6 20.4 %all-reduce.6.cloned.1.call-done = f32[8,128,512]{2,1,0:T(8,128)} async-done(((f32[8,128,512]{2,1,0:T(8,128)}), f32[8,128,512]{2,1,0:T(8,128)}) %all-reduce.6.cloned.1.call-update) | async-done | bytes 2097168 | tf_op jit(solution)/shard_map/psum | solution.py:15
  969.0 19.5 %fusion.3 = f32[16,1,128,8,1,128]{2,5,0,3,4,1:T(8,128)} fusion(f32[8,16,128,128]{2,3,1,0:T(8,128)} %copy.37, f32[16,128,8,128]{1,3,0,2:T(8,128)} %copy-done.5, pred[8]{0:T(512)(128)(4,1)S(1)} %get-tuple-element.88, pred[8]{0:T(512)(128)(4,1)S(1)} %get-tuple-element.89, pred[16,8]{0,1:T(8,128)(4,1)S(1)} %broadcast_and_fusion.1, ...), kind=kOutput, calls=%fused_computation.15 | convolution fusion | flops 12894863360 | bytes 31457520 | tf_op jit(solution)/shard_map/aik,cjk->aicj/dot_general | solution.py:139
  988.4 20.5 %copy.40 = f32[16,1,128,8,1,128]{5,4,3,2,1,0:T(1,128)} copy(f32[16,1,128,8,1,128]{2,5,0,3,4,1:T(8,128)} %fusion.3) | data formatting | bytes 16777216 | tf_op jit(solution)/shard_map/reshape | solution.py:148
  (221 shorter events, 372.3 us)
Async XLA Ops:
  6.5 303.0 %all-gather.5.cloned.1.call-start = ((), (), s32[]{:S(2)}) async-start(), calls=%async_computation.2 | async-start | bytes 1310720 | tf_op jit(solution)/shard_map/all_gather | solution.py:117
  122.8 3.4 copy-start.4
  126.2 46.7 %collective-permute-start = (f32[16,128,128]{1,2,0:T(8,128)S(1)}, f32[16,128,128]{1,2,0:T(8,128)S(1)}, u32[]{:S(2)}, u32[]{:S(2)}) collective-permute-start(f32[16,128,128]{1,2,0:T(8,128)S(1)} %slice_bitcast_fusion.1), channel_id=1, source_target_pairs={{0,1},{1,2},{2,3},{3,4},{4,5},{5,6},{6,7},{7,0},{8,9},{9,10},{10,1... | collective-permute-start | bytes 3145736 | tf_op jit(solution)/shard_map/ppermute | solution.py:100
  128.2 47.1 %collective-permute-start.1 = (f32[16,128,128]{1,2,0:T(8,128)S(1)}, f32[16,128,128]{1,2,0:T(8,128)S(1)}, u32[]{:S(2)}, u32[]{:S(2)}) collective-permute-start(f32[16,128,128]{1,2,0:T(8,128)S(1)} %slice_bitcast_fusion.1), channel_id=1, source_target_pairs={{0,7},{1,0},{2,1},{3,2},{4,3},{5,4},{6,5},{7,6},{8,15},{9,8},{10,9... | collective-permute-start | bytes 3145736 | tf_op jit(solution)/shard_map/ppermute | solution.py:105
  172.9 46.6 %collective-permute-start.2 = (f32[16,128,128]{1,2,0:T(8,128)S(1)}, f32[16,128,128]{1,2,0:T(8,128)S(1)}, u32[]{:S(2)}, u32[]{:S(2)}) collective-permute-start(f32[16,128,128]{1,2,0:T(8,128)S(1)} %collective-permute-done), channel_id=1, source_target_pairs={{0,1},{1,2},{2,3},{3,4},{4,5},{5,6},{6,7},{7,0},{8,9},{9,10},{10,1... | collective-permute-start | bytes 3145736 | tf_op jit(solution)/shard_map/ppermute | solution.py:100
  175.4 46.6 %collective-permute-start.3 = (f32[16,128,128]{1,2,0:T(8,128)S(1)}, f32[16,128,128]{1,2,0:T(8,128)}, u32[]{:S(2)}, u32[]{:S(2)}) collective-permute-start(f32[16,128,128]{1,2,0:T(8,128)S(1)} %collective-permute-done.1), channel_id=1, source_target_pairs={{0,7},{1,0},{2,1},{3,2},{4,3},{5,4},{6,5},{7,6},{8,15},{9,8},{10,9... | collective-permute-start | bytes 3145736 | tf_op jit(solution)/shard_map/ppermute | solution.py:105
  219.5 46.6 %collective-permute-start.4 = (f32[16,128,128]{1,2,0:T(8,128)S(1)}, f32[16,128,128]{1,2,0:T(8,128)}, u32[]{:S(2)}, u32[]{:S(2)}) collective-permute-start(f32[16,128,128]{1,2,0:T(8,128)S(1)} %collective-permute-done.2), channel_id=1, source_target_pairs={{0,1},{1,2},{2,3},{3,4},{4,5},{5,6},{6,7},{7,0},{8,9},{9,10},{10,1... | collective-permute-start | bytes 3145736 | tf_op jit(solution)/shard_map/ppermute | solution.py:100
  222.0 51.8 %collective-permute-start.5 = (f32[16,128,128]{1,2,0:T(8,128)}, f32[16,128,128]{1,2,0:T(8,128)}, u32[]{:S(2)}, u32[]{:S(2)}) collective-permute-start(f32[16,128,128]{1,2,0:T(8,128)} %collective-permute-done.3), channel_id=1, source_target_pairs={{0,7},{1,0},{2,1},{3,2},{4,3},{5,4},{6,5},{7,6},{8,15},{9,8},{10,9... | collective-permute-start | bytes 3145736 | tf_op jit(solution)/shard_map/ppermute | solution.py:105
  266.1 26.9 %collective-permute-start.6 = (f32[16,128,128]{1,2,0:T(8,128)}, f32[16,128,128]{1,2,0:T(8,128)S(1)}, u32[]{:S(2)}, u32[]{:S(2)}) collective-permute-start(f32[16,128,128]{1,2,0:T(8,128)} %collective-permute-done.4), channel_id=1, source_target_pairs={{0,1},{1,2},{2,3},{3,4},{4,5},{5,6},{6,7},{7,0},{8,9},{9,10},{10,1... | collective-permute-start | bytes 3145736 | tf_op jit(solution)/shard_map/ppermute | solution.py:100
  293.5 2.0 copy-start
  296.3 236.9 %all-reduce.4.cloned.1.call-start = ((), (), s32[]{:S(2)}) async-start(), calls=%async_computation | async-start | bytes 4194304 | tf_op jit(solution)/shard_map/psum | solution.py:15
  444.3 10.3 %copy-start.3 = (f32[16,128,512]{2,1,0:T(8,128)S(1)}, f32[16,128,512]{2,1,0:T(8,128)}, u32[]{:S(2)}) copy-start(f32[16,128,512]{2,1,0:T(8,128)} %copy.29) | copy-start | bytes 12582916
  481.6 264.2 %all-gather.7.cloned.1.call-start = ((), (), s32[]{:S(2)}) async-start(), calls=%async_computation.3 | async-start | bytes 1310720 | tf_op jit(solution)/shard_map/all_gather | solution.py:117
  559.4 3.4 copy-start.5
  562.9 46.2 %collective-permute-start.7 = (f32[16,128,128]{1,2,0:T(8,128)S(1)}, f32[16,128,128]{1,2,0:T(8,128)S(1)}, u32[]{:S(2)}, u32[]{:S(2)}) collective-permute-start(f32[16,128,128]{1,2,0:T(8,128)S(1)} %slice_bitcast_fusion), channel_id=1, source_target_pairs={{0,1},{1,2},{2,3},{3,4},{4,5},{5,6},{6,7},{7,0},{8,9},{9,10},{10,1... | collective-permute-start | bytes 3145736 | tf_op jit(solution)/shard_map/ppermute | solution.py:100
  564.4 47.1 %collective-permute-start.8 = (f32[16,128,128]{1,2,0:T(8,128)S(1)}, f32[16,128,128]{1,2,0:T(8,128)S(1)}, u32[]{:S(2)}, u32[]{:S(2)}) collective-permute-start(f32[16,128,128]{1,2,0:T(8,128)S(1)} %slice_bitcast_fusion), channel_id=1, source_target_pairs={{0,7},{1,0},{2,1},{3,2},{4,3},{5,4},{6,5},{7,6},{8,15},{9,8},{10,9... | collective-permute-start | bytes 3145736 | tf_op jit(solution)/shard_map/ppermute | solution.py:105
  609.1 46.3 %collective-permute-start.9 = (f32[16,128,128]{1,2,0:T(8,128)S(1)}, f32[16,128,128]{1,2,0:T(8,128)}, u32[]{:S(2)}, u32[]{:S(2)}) collective-permute-start(f32[16,128,128]{1,2,0:T(8,128)S(1)} %collective-permute-done.7), channel_id=1, source_target_pairs={{0,1},{1,2},{2,3},{3,4},{4,5},{5,6},{6,7},{7,0},{8,9},{9,10},{10,1... | collective-permute-start | bytes 3145736 | tf_op jit(solution)/shard_map/ppermute | solution.py:100
  611.6 46.4 %collective-permute-start.10 = (f32[16,128,128]{1,2,0:T(8,128)S(1)}, f32[16,128,128]{1,2,0:T(8,128)}, u32[]{:S(2)}, u32[]{:S(2)}) collective-permute-start(f32[16,128,128]{1,2,0:T(8,128)S(1)} %collective-permute-done.8), channel_id=1, source_target_pairs={{0,7},{1,0},{2,1},{3,2},{4,3},{5,4},{6,5},{7,6},{8,15},{9,8},{10,9... | collective-permute-start | bytes 3145736 | tf_op jit(solution)/shard_map/ppermute | solution.py:105
  655.3 46.1 %collective-permute-start.11 = (f32[16,128,128]{1,2,0:T(8,128)}, f32[16,128,128]{1,2,0:T(8,128)S(1)}, u32[]{:S(2)}, u32[]{:S(2)}) collective-permute-start(f32[16,128,128]{1,2,0:T(8,128)} %collective-permute-done.9), channel_id=1, source_target_pairs={{0,1},{1,2},{2,3},{3,4},{4,5},{5,6},{6,7},{7,0},{8,9},{9,10},{10,1... | collective-permute-start | bytes 3145736 | tf_op jit(solution)/shard_map/ppermute | solution.py:100
  657.9 50.9 %collective-permute-start.12 = (f32[16,128,128]{1,2,0:T(8,128)}, f32[16,128,128]{1,2,0:T(8,128)}, u32[]{:S(2)}, u32[]{:S(2)}) collective-permute-start(f32[16,128,128]{1,2,0:T(8,128)} %collective-permute-done.10), channel_id=1, source_target_pairs={{0,7},{1,0},{2,1},{3,2},{4,3},{5,4},{6,5},{7,6},{8,15},{9,8},{10,9... | collective-permute-start | bytes 3145736 | tf_op jit(solution)/shard_map/ppermute | solution.py:105
  701.4 26.2 %collective-permute-start.13 = (f32[16,128,128]{1,2,0:T(8,128)S(1)}, f32[16,128,128]{1,2,0:T(8,128)S(1)}, u32[]{:S(2)}, u32[]{:S(2)}) collective-permute-start(f32[16,128,128]{1,2,0:T(8,128)S(1)} %collective-permute-done.11), channel_id=1, source_target_pairs={{0,1},{1,2},{2,3},{3,4},{4,5},{5,6},{6,7},{7,0},{8,9},{9,10},{10,1... | collective-permute-start | bytes 3145736 | tf_op jit(solution)/shard_map/ppermute | solution.py:100
  728.1 2.0 copy-start.1
  730.8 238.1 %all-reduce.6.cloned.1.call-start = ((), (), s32[]{:S(2)}) async-start(), calls=%async_computation.1 | async-start | bytes 4194304 | tf_op jit(solution)/shard_map/psum | solution.py:15
  880.4 10.3 %copy-start.2 = (f32[16,128,512]{2,1,0:T(8,128)S(1)}, f32[16,128,512]{2,1,0:T(8,128)}, u32[]{:S(2)}) copy-start(f32[16,128,512]{2,1,0:T(8,128)} %copy.35) | copy-start | bytes 12582916
Sparse Core Ops, SparseCore 0:
  296.4 13.1 all-gather.4
  481.7 51.3 all-reduce.3
  731.0 14.7 all-gather.6
  917.5 51.3 all-reduce.5
